TPU v7x, 512 devices: a whole 4x8x8 slice. The times are simulated.
512 devices in a mesh: energy: 32 (over x, z_hi, core), cuts: 16 (over z_lo, y).
Axes of the slice: x: 4, y: 8, z: 8 (z_hi: 4, z_lo: 2; z = z_hi * 2 + z_lo), core: 2. Of those that a mesh axis runs over, the one named last changes fastest.
Arguments:
- green_diag: bfloat16 [16, 128, 2, 256, 256], P('cuts', 'energy'), may hold values from -0.375 to 0.375
- green_upper: bfloat16 [16, 128, 2, 256, 256], P('cuts', 'energy'), may hold values from -0.375 to 0.375
- sigma_lesser: bfloat16 [16, 128, 2, 256, 256], P('cuts', 'energy'), may hold values from -6 to 6
- screening: bfloat16 [16, 128, 2, 256, 256], P('cuts', 'energy'), may hold values from -0.375 to 0.375
Outputs:
- polar_screened: bfloat16 [16, 128, 2, 256, 256], P('cuts', 'energy')
All inputs are finite; a program needn't handle non-finite values.
Results may differ from a plain program's by a relative error of at most 0.013.
Values may be sent and summed in bfloat16 or wider, within the bound.
No kernel may reach another device: no remote copies, remote signals or barrier semaphores. Data moves between devices by JAX's collectives and lax.ppermute only.
A program may use at most 64 MiB of HBM per device.

v0:
```python
import math
import jax
import jax.numpy as jnp
from jax import lax
from jax.sharding import PartitionSpec as P


def shifted(value, axis, steps):
    count = lax.axis_size(axis)
    leading, last = (max(0, -steps), min(count, count - steps))
    return lax.ppermute(value, axis, [(source, source + steps) for source in range(leading, last)])


def times_block(left, right):
    real = jnp.einsum(
        "eij,ejk->eik", left[:, 0], right[:, 0], preferred_element_type=jnp.float32
    ) - jnp.einsum("eij,ejk->eik", left[:, 1], right[:, 1], preferred_element_type=jnp.float32)
    imag = jnp.einsum(
        "eij,ejk->eik", left[:, 0], right[:, 1], preferred_element_type=jnp.float32
    ) + jnp.einsum("eij,ejk->eik", left[:, 1], right[:, 0], preferred_element_type=jnp.float32)
    return jnp.stack([real, imag], axis=1)


def times_adjoint(left, right):
    real = jnp.einsum(
        "eij,ekj->eik", left[:, 0], right[:, 0], preferred_element_type=jnp.float32
    ) + jnp.einsum("eij,ekj->eik", left[:, 1], right[:, 1], preferred_element_type=jnp.float32)
    imag = jnp.einsum(
        "eij,ekj->eik", left[:, 1], right[:, 0], preferred_element_type=jnp.float32
    ) - jnp.einsum("eij,ekj->eik", left[:, 0], right[:, 1], preferred_element_type=jnp.float32)
    return jnp.stack([real, imag], axis=1)


def angle_table(rows_count, cols_count, period):
    row_index = lax.broadcasted_iota(jnp.int32, (rows_count, cols_count), 0)
    col_index = lax.broadcasted_iota(jnp.int32, (rows_count, cols_count), 1)
    phase = (row_index * col_index % period).astype(jnp.float32)
    return phase * (2.0 * math.pi / period)


def split_table_dot(table, data):
    upper = table.astype(jnp.bfloat16)
    lower = (table - upper.astype(jnp.float32)).astype(jnp.bfloat16)
    return jnp.dot(upper, data, preferred_element_type=jnp.float32) + jnp.dot(
        lower, data, preferred_element_type=jnp.float32
    )


def correlate(spread):
    energies = spread.shape[0]
    period = 2 * energies
    forward = angle_table(period, energies, period)
    inverse = angle_table(energies, period, period)
    cos_inv = jnp.cos(inverse)
    sin_inv = jnp.sin(inverse)
    real_part = spread[:, 0].reshape(energies, -1)
    imag_part = spread[:, 1].reshape(energies, -1)
    width = real_part.shape[1]
    joined = jnp.concatenate([real_part, imag_part], axis=1)
    cos_both = split_table_dot(jnp.cos(forward), joined)
    sin_both = split_table_dot(jnp.sin(forward), joined)
    spec_real = cos_both[:, :width] + sin_both[:, width:]
    spec_imag = cos_both[:, width:] - sin_both[:, :width]
    power = spec_real * spec_real + spec_imag * spec_imag
    lag_real = jnp.dot(cos_inv, power) / period
    lag_imag = jnp.dot(sin_inv, power) / period
    polar = jnp.stack([lag_real, lag_imag], axis=1) / energies
    return polar.reshape(spread.shape).astype(jnp.bfloat16)


def shards(green_diag, green_upper, sigma_lesser, screening):
    sigma_next = shifted(sigma_lesser, "cuts", -1)
    own_term = times_block(green_diag[0], sigma_lesser[0]).astype(jnp.bfloat16)
    pair_term = times_block(green_upper[0], sigma_next[0]).astype(jnp.bfloat16)
    lesser = (
        times_adjoint(own_term, green_diag[0]) + times_adjoint(pair_term, green_upper[0])
    ).astype(jnp.bfloat16)
    entries = lax.all_to_all(lesser, "energy", split_axis=2, concat_axis=0, tiled=True)
    polar_rows = correlate(entries)
    back_field = lax.all_to_all(polar_rows, "energy", split_axis=0, concat_axis=2, tiled=True)
    screened_left = times_block(screening[0], back_field).astype(jnp.bfloat16)
    result_field = times_adjoint(screened_left, screening[0]).astype(jnp.bfloat16)
    return result_field[None]


def solution(mesh):
    in_specs = (
        P("cuts", "energy", None, None, None),
        P("cuts", "energy", None, None, None),
        P("cuts", "energy", None, None, None),
        P("cuts", "energy", None, None, None),
    )
    out_specs = P("cuts", "energy", None, None, None)
    return jax.shard_map(shards, mesh=mesh, in_specs=in_specs, out_specs=out_specs, check_vma=False)
```

profile of v0, /device:TPU:57, one launch (start us, length us, event | category | flops | bytes accessed | tf_op | source)
XLA Modules:
  0.0 122.9 jit_solution(17262940203430919250)
XLA Ops:
  0.0 0.0 copy-start
  0.0 1.4 %copy.101 = bf16[1,4,2,256,256]{4,3,1,2,0:T(8,128)(2,1)S(1)} copy(bf16[1,4,2,256,256]{4,3,2,1,0:T(8,128)(2,1)} %param.6) | data formatting | bytes 2097152 | tf_op args[2]
  1.4 3.0 %collective-permute-start = (bf16[1,4,2,256,256]{4,3,1,2,0:T(8,128)(2,1)S(1)}, bf16[1,4,2,256,256]{4,3,1,2,0:T(8,128)(2,1)S(1)}, u32[]{:S(2)}, u32[]{:S(2)}) collective-permute-start(bf16[1,4,2,256,256]{4,3,1,2,0:T(8,128)(2,1)S(1)} %copy.101), channel_id=1, source_target_pairs={{1,0},{2,1},{3,2},{4,3},{5,4},{6,5},{7,6},{8,7},{9,8},{10,9},{11,1... | collective-permute-start | bytes 3145736 | tf_op jit(solution)/shard_map/ppermute | solution.py:11
  4.4 0.0 copy-done
  4.4 0.1 copy.100
  4.5 0.3 fusion.19
  4.8 0.3 fusion.20
  5.1 0.0 copy-start.1
  5.1 0.3 fusion.9
  5.4 0.3 fusion.26
  5.7 0.6 copy-done.1
  6.3 0.1 copy.99
  6.4 0.3 fusion.10
  6.7 0.3 fusion.8
  7.0 0.3 fusion.25
  7.4 0.3 fusion.7
  7.7 21.7 %collective-permute-done = bf16[1,4,2,256,256]{4,3,1,2,0:T(8,128)(2,1)S(1)} collective-permute-done((bf16[1,4,2,256,256]{4,3,1,2,0:T(8,128)(2,1)S(1)}, bf16[1,4,2,256,256]{4,3,1,2,0:T(8,128)(2,1)S(1)}, u32[]{:S(2)}, u32[]{:S(2)}) %collective-permute-start) | collective-permute-done | bytes 1048608 | tf_op jit(solution)/shard_map/ppermute | solution.py:11
  29.4 0.3 fusion.22
  29.7 0.3 fusion.21
  30.0 0.3 fusion.11
  30.4 0.3 fusion.28
  30.7 0.3 fusion.12
  31.0 0.3 fusion.27
  31.3 0.3 fusion.6
  31.7 0.3 fusion.5
  32.0 0.4 fusion.3
  32.5 0.8 copy.65
  33.3 42.2 %all_to_all.36 = bf16[4,2,256,256]{3,0,1,2:T(4,128)(2,1)S(1)} all-to-all(bf16[4,2,256,256]{3,0,1,2:T(4,128)(2,1)S(1)} %copy.65), channel_id=1, replica_groups=mesh['energy'=32,'cuts'=16] {'energy'}, dimensions={2} | all-to-all | bytes 2097152 | tf_op jit(solution)/shard_map/all_to_all | solution.py:78
  75.5 0.2 copy.98
  75.7 0.1 copy.67
  75.9 0.1 fusion.83
  75.9 0.1 copy.85
  76.1 0.1 copy.86
  76.3 1.1 fusion.55
  77.4 1.1 fusion.52
  78.5 1.1 convolution_add_fusion.1
  79.7 1.1 convolution_add_fusion
  80.8 0.9 fusion.1
  81.7 0.8 convolution_multiply_fusion.1
  82.5 0.8 convolution_multiply_fusion
  83.3 0.3 copy.87
  83.6 0.3 copy.88
  84.0 0.0 copy-start.2
  84.0 1.2 fusion.4
  85.1 4.9 %all-to-all-start.1 = ((bf16[128,2,8,256]{3,2,1,0:T(8,128)(2,1)}), bf16[128,2,8,256]{3,2,1,0:T(8,128)(2,1)S(1)}, u32[]{:S(2)}, u32[]{:S(2)}) async-start(bf16[128,2,8,256]{3,2,1,0:T(8,128)(2,1)} %fusion.4), calls=%async_computation.1 | async-start | bytes 2097152 | tf_op jit(solution)/shard_map/all_to_all | solution.py:80
  90.1 0.0 copy-done.2
  90.1 0.1 copy.96
  90.2 28.7 %all-to-all-done.1 = bf16[128,2,8,256]{3,2,1,0:T(8,128)(2,1)S(1)} async-done(((bf16[128,2,8,256]{3,2,1,0:T(8,128)(2,1)}), bf16[128,2,8,256]{3,2,1,0:T(8,128)(2,1)S(1)}, u32[]{:S(2)}, u32[]{:S(2)}) %all-to-all-start.1) | async-done | bytes 1048608 | tf_op jit(solution)/shard_map/all_to_all | solution.py:80
  118.9 0.1 copy.97
  118.9 0.4 fusion.23
  119.3 0.3 fusion.24
  119.6 0.3 fusion.13
  120.0 0.3 fusion.30
  120.3 0.4 fusion.14
  120.7 0.3 fusion.29
  121.0 0.3 fusion.18
  121.4 0.3 fusion.17
  121.7 0.1 pad_maximum_fusion
  121.9 1.0 copy.78
  (2 shorter events, 0.1 us)
Async XLA Ops:
  0.0 4.4 %copy-start = (bf16[1,4,2,256,256]{4,3,2,1,0:T(8,128)(2,1)S(1)}, bf16[1,4,2,256,256]{4,3,2,1,0:T(8,128)(2,1)}, u32[]{:S(2)}) copy-start(bf16[1,4,2,256,256]{4,3,2,1,0:T(8,128)(2,1)} %param.4) | copy-start | bytes 3145732
  1.4 28.0 %collective-permute-start = (bf16[1,4,2,256,256]{4,3,1,2,0:T(8,128)(2,1)S(1)}, bf16[1,4,2,256,256]{4,3,1,2,0:T(8,128)(2,1)S(1)}, u32[]{:S(2)}, u32[]{:S(2)}) collective-permute-start(bf16[1,4,2,256,256]{4,3,1,2,0:T(8,128)(2,1)S(1)} %copy.101), channel_id=1, source_target_pairs={{1,0},{2,1},{3,2},{4,3},{5,4},{6,5},{7,6},{8,7},{9,8},{10,9},{11,1... | collective-permute-start | bytes 3145736 | tf_op jit(solution)/shard_map/ppermute | solution.py:11
  5.1 1.2 copy-start.1
  84.0 6.1 %copy-start.2 = (bf16[1,4,2,256,256]{4,3,2,1,0:T(8,128)(2,1)S(1)}, bf16[1,4,2,256,256]{4,3,2,1,0:T(8,128)(2,1)}, u32[]{:S(2)}) copy-start(bf16[1,4,2,256,256]{4,3,2,1,0:T(8,128)(2,1)} %param.7) | copy-start | bytes 3145732
  85.1 33.7 %all-to-all-start.1 = ((bf16[128,2,8,256]{3,2,1,0:T(8,128)(2,1)}), bf16[128,2,8,256]{3,2,1,0:T(8,128)(2,1)S(1)}, u32[]{:S(2)}, u32[]{:S(2)}) async-start(bf16[128,2,8,256]{3,2,1,0:T(8,128)(2,1)} %fusion.4), calls=%async_computation.1 | async-start | bytes 2097152 | tf_op jit(solution)/shard_map/all_to_all | solution.py:80
where the time goes:
time: 123 us
  waiting for transfers between devices  50.4 us (41%)
  blocking collectives  42.2 us (34%)
  matrix products  13.9 us (11%)
  starting transfers between devices  7.91 us (6%)
  local copies, waits for them, and re-layouts  5.47 us (4%)
  other arithmetic  2.62 us (2%)
    all_to_all x1, blocking collectives, shards(): lax.all_to_all(lesser, 'energy', split_axis=2, concat_axis=0, tiled=True)  42.2 us
    all_to_all x1, waiting for transfers between devices, shards(): lax.all_to_all(polar_rows, 'energy', split_axis=0, concat_axis=2, tiled=T...  28.7 us
    ppermute x1, waiting for transfers between devices, shifted(): lax.ppermute(value, axis, [(source, source + steps) for source in range(l...  21.7 us
    all_to_all x1, starting transfers between devices, shards(): lax.all_to_all(polar_rows, 'energy', split_axis=0, concat_axis=2, tiled=T...  4.93 us
    unnamed x15, local copies, waits for them, and re-layouts  3.11 us
    ppermute x1, starting transfers between devices, shifted(): lax.ppermute(value, axis, [(source, source + steps) for source in range(l...  2.98 us
  transfers between devices with their start and end apart: 2, of which 2 were waited for; matrix products, arithmetic and copies ran while one was open for 2% of the time, Pallas kernels for 0%

commit v1 on v0

--- a/solution.py
+++ b/solution.py
@@ -75,7 +75,10 @@
     lesser = (
         times_adjoint(own_term, green_diag[0]) + times_adjoint(pair_term, green_upper[0])
     ).astype(jnp.bfloat16)
-    entries = lax.all_to_all(lesser, "energy", split_axis=2, concat_axis=0, tiled=True)
+    n_dev = lax.axis_size("energy")
+    blocks = jnp.stack(jnp.split(lesser, n_dev, axis=2), axis=0)
+    blocks = lax.all_to_all(blocks, "energy", split_axis=0, concat_axis=0)
+    entries = jnp.concatenate(blocks, axis=0)
     polar_rows = correlate(entries)
     back_field = lax.all_to_all(polar_rows, "energy", split_axis=0, concat_axis=2, tiled=True)
     screened_left = times_block(screening[0], back_field).astype(jnp.bfloat16)

time: 123 us -> 123 us (level)
    unnamed x15 -> x46, local copies, waits for them, and re-layouts: 3.11 us -> 3.33 us
where the time goes in v1:
time: 123 us; the launch traced here: 122 us
  waiting for transfers between devices  50.5 us (41%)
  blocking collectives  42.2 us (34%)
  matrix products  13.8 us (11%)
  starting transfers between devices  7.9 us (6%)
  local copies, waits for them, and re-layouts  4.64 us (4%)
  other arithmetic  2.62 us (2%)
    all_to_all x1, blocking collectives, shards(): blocks = lax.all_to_all(blocks, 'energy', split_axis=0, concat_axis=0)  42.2 us
    all_to_all x1, waiting for transfers between devices, shards(): lax.all_to_all(polar_rows, 'energy', split_axis=0, concat_axis=2, tiled=T...  28.7 us
    ppermute x1, waiting for transfers between devices, shifted(): lax.ppermute(value, axis, [(source, source + steps) for source in range(l...  21.7 us
    all_to_all x1, starting transfers between devices, shards(): lax.all_to_all(polar_rows, 'energy', split_axis=0, concat_axis=2, tiled=T...  4.92 us
    unnamed x46, local copies, waits for them, and re-layouts  3.33 us
    ppermute x1, starting transfers between devices, shifted(): lax.ppermute(value, axis, [(source, source + steps) for source in range(l...  2.98 us
  transfers between devices with their start and end apart: 2, of which 2 were waited for; matrix products, arithmetic and copies ran while one was open for 2% of the time, Pallas kernels for 0%

profile of v1, /device:TPU:57, one launch (start us, length us, event | category | flops | bytes accessed | tf_op | source)
XLA Modules:
  0.0 122.3 jit_solution(18437387593843449315)
XLA Ops:
  0.0 0.0 copy-start
  0.0 1.4 %copy.65 = bf16[1,4,2,256,256]{4,3,1,2,0:T(8,128)(2,1)S(1)} copy(bf16[1,4,2,256,256]{4,3,2,1,0:T(8,128)(2,1)} %param.6) | data formatting | bytes 2097152 | tf_op args[2]
  1.4 3.0 %collective-permute-start = (bf16[1,4,2,256,256]{4,3,1,2,0:T(8,128)(2,1)S(1)}, bf16[1,4,2,256,256]{4,3,1,2,0:T(8,128)(2,1)S(1)}, u32[]{:S(2)}, u32[]{:S(2)}) collective-permute-start(bf16[1,4,2,256,256]{4,3,1,2,0:T(8,128)(2,1)S(1)} %copy.65), channel_id=1, source_target_pairs={{1,0},{2,1},{3,2},{4,3},{5,4},{6,5},{7,6},{8,7},{9,8},{10,9},{11,1... | collective-permute-start | bytes 3145736 | tf_op jit(solution)/shard_map/ppermute | solution.py:11
  4.4 0.0 copy-done
  4.4 0.1 copy.64
  4.5 0.3 fusion.19
  4.8 0.3 fusion.20
  5.1 0.0 copy-start.1
  5.1 0.3 fusion.9
  5.4 0.3 fusion.26
  5.7 0.6 copy-done.1
  6.3 0.1 copy.63
  6.4 0.3 fusion.10
  6.7 0.3 fusion.8
  7.0 0.3 fusion.25
  7.4 0.3 fusion.7
  7.7 21.7 %collective-permute-done = bf16[1,4,2,256,256]{4,3,1,2,0:T(8,128)(2,1)S(1)} collective-permute-done((bf16[1,4,2,256,256]{4,3,1,2,0:T(8,128)(2,1)S(1)}, bf16[1,4,2,256,256]{4,3,1,2,0:T(8,128)(2,1)S(1)}, u32[]{:S(2)}, u32[]{:S(2)}) %collective-permute-start) | collective-permute-done | bytes 1048608 | tf_op jit(solution)/shard_map/ppermute | solution.py:11
  29.4 0.3 fusion.22
  29.7 0.3 fusion.21
  30.0 0.3 fusion.11
  30.4 0.3 fusion.28
  30.7 0.3 fusion.12
  31.0 0.3 fusion.27
  31.3 0.3 fusion.6
  31.7 0.3 fusion.5
  32.0 0.4 fusion.3
  32.9 42.2 %all_to_all.23 = bf16[32,4,2,8,256]{4,3,1,2,0:T(8,128)(2,1)S(1)} all-to-all(bf16[32,4,2,8,256]{4,3,1,2,0:T(8,128)(2,1)S(1)} %constant_dynamic-update-slice_fusion), channel_id=1, replica_groups=mesh['energy'=32,'cuts'=16] {'energy'}, dimensions={0} | all-to-all | bytes 2097152 | tf_op jit(solution)/shard_map/all_to_all | solution.py:80
  75.2 0.1 copy.33
  75.3 0.1 fusion.83
  75.3 0.1 copy.51
  75.5 0.1 copy.52
  75.7 1.1 fusion.55
  76.8 1.1 fusion.52
  77.9 1.1 convolution_add_fusion.1
  79.1 1.1 convolution_add_fusion
  80.2 0.9 fusion.1
  81.1 0.8 convolution_multiply_fusion.1
  81.9 0.8 convolution_multiply_fusion
  82.7 0.3 copy.53
  83.0 0.3 copy.54
  83.4 0.0 copy-start.2
  83.4 1.2 fusion.4
  84.5 4.9 %all-to-all-start.1 = ((bf16[128,2,8,256]{3,2,1,0:T(8,128)(2,1)}), bf16[128,2,8,256]{3,2,1,0:T(8,128)(2,1)S(1)}, u32[]{:S(2)}, u32[]{:S(2)}) async-start(bf16[128,2,8,256]{3,2,1,0:T(8,128)(2,1)} %fusion.4), calls=%async_computation.1 | async-start | bytes 2097152 | tf_op jit(solution)/shard_map/all_to_all | solution.py:83
  89.5 0.0 copy-done.2
  89.5 0.1 copy.61
  89.6 28.7 %all-to-all-done.1 = bf16[128,2,8,256]{3,2,1,0:T(8,128)(2,1)S(1)} async-done(((bf16[128,2,8,256]{3,2,1,0:T(8,128)(2,1)}), bf16[128,2,8,256]{3,2,1,0:T(8,128)(2,1)S(1)}, u32[]{:S(2)}, u32[]{:S(2)}) %all-to-all-start.1) | async-done | bytes 1048608 | tf_op jit(solution)/shard_map/all_to_all | solution.py:83
  118.3 0.1 copy.62
  118.4 0.3 fusion.23
  118.7 0.3 fusion.24
  119.0 0.3 fusion.13
  119.4 0.3 fusion.30
  119.7 0.3 fusion.14
  120.1 0.3 fusion.29
  120.4 0.3 fusion.18
  120.8 0.3 fusion.17
  121.1 0.1 pad_maximum_fusion
  121.2 1.0 copy.44
  (34 shorter events, 0.3 us)
Async XLA Ops:
  0.0 4.4 %copy-start = (bf16[1,4,2,256,256]{4,3,2,1,0:T(8,128)(2,1)S(1)}, bf16[1,4,2,256,256]{4,3,2,1,0:T(8,128)(2,1)}, u32[]{:S(2)}) copy-start(bf16[1,4,2,256,256]{4,3,2,1,0:T(8,128)(2,1)} %param.4) | copy-start | bytes 3145732
  1.4 28.0 %collective-permute-start = (bf16[1,4,2,256,256]{4,3,1,2,0:T(8,128)(2,1)S(1)}, bf16[1,4,2,256,256]{4,3,1,2,0:T(8,128)(2,1)S(1)}, u32[]{:S(2)}, u32[]{:S(2)}) collective-permute-start(bf16[1,4,2,256,256]{4,3,1,2,0:T(8,128)(2,1)S(1)} %copy.65), channel_id=1, source_target_pairs={{1,0},{2,1},{3,2},{4,3},{5,4},{6,5},{7,6},{8,7},{9,8},{10,9},{11,1... | collective-permute-start | bytes 3145736 | tf_op jit(solution)/shard_map/ppermute | solution.py:11
  5.1 1.2 %copy-start.1 = (bf16[1,4,2,256,256]{4,3,2,1,0:T(8,128)(2,1)S(1)}, bf16[1,4,2,256,256]{4,3,2,1,0:T(8,128)(2,1)}, u32[]{:S(2)}) copy-start(bf16[1,4,2,256,256]{4,3,2,1,0:T(8,128)(2,1)} %param.5) | copy-start | bytes 3145732
  83.4 6.1 %copy-start.2 = (bf16[1,4,2,256,256]{4,3,2,1,0:T(8,128)(2,1)S(1)}, bf16[1,4,2,256,256]{4,3,2,1,0:T(8,128)(2,1)}, u32[]{:S(2)}) copy-start(bf16[1,4,2,256,256]{4,3,2,1,0:T(8,128)(2,1)} %param.7) | copy-start | bytes 3145732
  84.5 33.7 %all-to-all-start.1 = ((bf16[128,2,8,256]{3,2,1,0:T(8,128)(2,1)}), bf16[128,2,8,256]{3,2,1,0:T(8,128)(2,1)S(1)}, u32[]{:S(2)}, u32[]{:S(2)}) async-start(bf16[128,2,8,256]{3,2,1,0:T(8,128)(2,1)} %fusion.4), calls=%async_computation.1 | async-start | bytes 2097152 | tf_op jit(solution)/shard_map/all_to_all | solution.py:83
